TPU v7x, 256 devices: a whole 4x4x8 slice. The times are simulated.
256 devices in a mesh: row: 16 (over z, core), col: 16 (over x, y).
Axes of the slice: x: 4, y: 4, z: 8, core: 2. Of those that a mesh axis runs over, the one named last changes fastest.
Arguments:
- rhs: float32 [16, 64, 128], P('col'), may hold values from -6 to 6
- diag_inv: float32 [16, 128, 128], P('col'), as said below
- panel: bfloat16 [16, 16, 128, 128], P('row', 'col'), may hold values from -0.09375 to 0.09375
- offdiag: bfloat16 [1024, 16, 128, 128], P('row', 'col'), may hold values from -0.015625 to 0.015625
- known: bfloat16 [512, 64, 128], P(('row', 'col')), may hold values from -6 to 6
- row_index: int32 [1024], P('row'), may hold values from 0 to 31
Outputs:
- solution: bfloat16 [16, 64, 128], P('col')
Inputs may be any that keep to these rules, and one draw needn't show every extreme that they name: Each block of diag_inv is lower triangular (the inverse of a lower triangular diagonal block).
All inputs are finite; a program needn't handle non-finite values.
Results may differ from a plain program's by a relative error of at most 0.015.
Values may be sent and summed in bfloat16 or wider, within the bound.
A program may use at most 64 MiB of HBM per device.

v0:
```python
import jax
import jax.numpy as jnp
from jax import lax
from jax.sharding import PartitionSpec as P

NB = 16


def spread(array, axis, root):
    mine = lax.axis_index(axis) == root
    return lax.psum(jnp.where(mine, array, jnp.zeros_like(array)), axis)


def finish_block(total, inverse, turn_block, root, solved):
    local = jnp.dot(
        total, inverse, precision=lax.Precision.HIGHEST, preferred_element_type=jnp.float32
    ).astype(jnp.bfloat16)
    block = spread(local, "col", root)
    solved = lax.dynamic_update_index_in_dim(solved, block, turn_block, 0)
    return (block, solved)


def body(rhs, diag_inv, panel, offdiag, known, row_index):
    rows_count = lax.axis_size("row")
    cols_count = lax.axis_size("col")
    row_id = lax.axis_index("row")
    col_id = lax.axis_index("col")
    col_slots = NB // cols_count
    known_row = lax.all_gather(known, "col", axis=0, tiled=True)
    picked = jnp.take(known_row, row_index, axis=0)
    off_part = jnp.einsum("pqi,pbia->bqa", picked, offdiag, preferred_element_type=jnp.float32)
    off_sum = lax.psum(off_part, "row")
    update = rhs - off_sum
    col_global = jnp.arange(col_slots) * cols_count + col_id
    accum = jnp.zeros(update.shape, jnp.float32)
    solved = jnp.zeros((NB,) + update.shape[1:], jnp.bfloat16)

    def step_reduced(turn, carry):
        sums, result = carry
        block_id = NB - 1 - turn
        slot = block_id // cols_count
        partial_value = lax.dynamic_index_in_dim(sums, slot, 0, keepdims=False)
        summed = lax.psum(partial_value.astype(jnp.bfloat16), "row").astype(jnp.float32)
        total = lax.dynamic_index_in_dim(update, slot, 0, keepdims=False) - summed
        inverse = lax.dynamic_index_in_dim(diag_inv, slot, 0, keepdims=False)
        block, result = finish_block(total, inverse, block_id, block_id % cols_count, result)
        tiles = lax.dynamic_index_in_dim(panel, block_id // rows_count, 0, keepdims=False)
        contrib = jnp.einsum("qi,bia->bqa", block, tiles, preferred_element_type=jnp.float32)
        keep = (col_global < block_id) & (block_id % rows_count == row_id)
        return (sums + jnp.where(keep[:, None, None], contrib, 0.0), result)

    accum, solved = lax.fori_loop(0, NB, step_reduced, (accum, solved))
    return jnp.take(solved, col_global, axis=0)


def solution(mesh):
    placed = (
        P("col", None, None),
        P("col", None, None),
        P("row", "col", None, None),
        P("row", "col", None, None),
        P(("row", "col"), None, None),
        P("row"),
    )
    return jax.shard_map(
        body, mesh=mesh, in_specs=placed, out_specs=P("col", None, None), check_vma=False
    )
```

profile of v0, /device:TPU:1, one launch (start us, length us, event | category | flops | bytes accessed | tf_op | source)
XLA Modules:
  0.0 1914.5 jit_solution(12652828160161664547)
XLA Ops:
  0.0 20.1 %all_gather.3 = bf16[32,64,128]{2,1,0:T(8,128)(2,1)S(1)} all-gather(bf16[2,64,128]{2,1,0:T(8,128)(2,1)} %param.12), channel_id=1, replica_groups=mesh['row'=16,'col'=16] {'col'}, dimensions={0}, use_global_device_ids=true | all-gather | bytes 557056 | tf_op jit(solution)/shard_map/all_gather | solution.py:29
  20.1 0.7 compare_select_fusion
  20.8 1.7 gather_fusion
  22.5 1.8 fusion.9
  24.3 50.9 %psum.35 = f32[1,64,128]{2,1,0:T(8,128)S(1)} all-reduce(f32[1,64,128]{2,1,0:T(8,128)S(1)} %fusion.9), channel_id=1, replica_groups=mesh['row'=16,'col'=16] {'row'}, use_global_device_ids=true, to_apply=%region_0.1 | all-reduce | flops 8192 | bytes 65536 | tf_op jit(solution)/shard_map/psum | solution.py:32
  75.3 1838.6 %while.19 = (s32[]{:T(128)}, f32[1,64,128]{2,1,0:T(8,128)S(1)}, bf16[16,64,128]{2,1,0:T(8,128)(2,1)S(1)}, s32[1]{0:T(128)}, s32[]{:T(128)}, /*index=5*/f32[1,64,...) while((s32[]{:T(128)}, f32[1,64,128]{2,1,0:T(8,128)S(1)}, ...), condition=%wide.region_4.5_spmd.clone, body=%wide.region_1.0_spmd.clone.sunk | while | flops 14762007 | bytes 393562 | solution.py:52
  75.3 45.7 %psum.40 = bf16[64,128]{1,0:T(8,128)(2,1)S(1)} all-reduce(bf16[64,128]{1,0:T(8,128)(2,1)S(1)} %fusion.26), channel_id=1, replica_groups=mesh['row'=16,'col'=16] {'row'}, use_global_device_ids=true, to_apply=%region_2.2 | all-reduce | flops 8192 | bytes 32768 | tf_op jit(solution)/shard_map/while/body/eval_jaxpr/psum | solution.py:43
  121.1 0.2 fusion.27
  121.2 58.2 %psum.41 = bf16[64,128]{1,0:T(8,128)(2,1)S(1)} all-reduce(bf16[64,128]{1,0:T(8,128)(2,1)S(1)} %fusion.27), channel_id=1, replica_groups=mesh['row'=16,'col'=16] {'col'}, use_global_device_ids=true, to_apply=%region_3.3 | all-reduce | flops 8192 | bytes 32768 | tf_op jit(solution)/shard_map/while/body/eval_jaxpr/psum | solution.py:11
  179.5 0.1 fusion.28
  179.6 59.6 %psum.40 = bf16[64,128]{1,0:T(8,128)(2,1)S(1)} all-reduce(bf16[64,128]{1,0:T(8,128)(2,1)S(1)} %fusion.26), channel_id=1, replica_groups=mesh['row'=16,'col'=16] {'row'}, use_global_device_ids=true, to_apply=%region_2.2 | all-reduce | flops 8192 | bytes 32768 | tf_op jit(solution)/shard_map/while/body/eval_jaxpr/psum | solution.py:43
  239.2 0.2 fusion.27
  239.4 55.7 %psum.41 = bf16[64,128]{1,0:T(8,128)(2,1)S(1)} all-reduce(bf16[64,128]{1,0:T(8,128)(2,1)S(1)} %fusion.27), channel_id=1, replica_groups=mesh['row'=16,'col'=16] {'col'}, use_global_device_ids=true, to_apply=%region_3.3 | all-reduce | flops 8192 | bytes 32768 | tf_op jit(solution)/shard_map/while/body/eval_jaxpr/psum | solution.py:11
  295.1 0.1 fusion.28
  295.2 59.6 %psum.40 = bf16[64,128]{1,0:T(8,128)(2,1)S(1)} all-reduce(bf16[64,128]{1,0:T(8,128)(2,1)S(1)} %fusion.26), channel_id=1, replica_groups=mesh['row'=16,'col'=16] {'row'}, use_global_device_ids=true, to_apply=%region_2.2 | all-reduce | flops 8192 | bytes 32768 | tf_op jit(solution)/shard_map/while/body/eval_jaxpr/psum | solution.py:43
  354.8 0.2 fusion.27
  355.0 55.7 %psum.41 = bf16[64,128]{1,0:T(8,128)(2,1)S(1)} all-reduce(bf16[64,128]{1,0:T(8,128)(2,1)S(1)} %fusion.27), channel_id=1, replica_groups=mesh['row'=16,'col'=16] {'col'}, use_global_device_ids=true, to_apply=%region_3.3 | all-reduce | flops 8192 | bytes 32768 | tf_op jit(solution)/shard_map/while/body/eval_jaxpr/psum | solution.py:11
  410.9 59.6 %psum.40 = bf16[64,128]{1,0:T(8,128)(2,1)S(1)} all-reduce(bf16[64,128]{1,0:T(8,128)(2,1)S(1)} %fusion.26), channel_id=1, replica_groups=mesh['row'=16,'col'=16] {'row'}, use_global_device_ids=true, to_apply=%region_2.2 | all-reduce | flops 8192 | bytes 32768 | tf_op jit(solution)/shard_map/while/body/eval_jaxpr/psum | solution.py:43
  470.4 0.2 fusion.27
  470.6 55.7 %psum.41 = bf16[64,128]{1,0:T(8,128)(2,1)S(1)} all-reduce(bf16[64,128]{1,0:T(8,128)(2,1)S(1)} %fusion.27), channel_id=1, replica_groups=mesh['row'=16,'col'=16] {'col'}, use_global_device_ids=true, to_apply=%region_3.3 | all-reduce | flops 8192 | bytes 32768 | tf_op jit(solution)/shard_map/while/body/eval_jaxpr/psum | solution.py:11
  526.3 0.1 fusion.28
  526.5 59.6 %psum.40 = bf16[64,128]{1,0:T(8,128)(2,1)S(1)} all-reduce(bf16[64,128]{1,0:T(8,128)(2,1)S(1)} %fusion.26), channel_id=1, replica_groups=mesh['row'=16,'col'=16] {'row'}, use_global_device_ids=true, to_apply=%region_2.2 | all-reduce | flops 8192 | bytes 32768 | tf_op jit(solution)/shard_map/while/body/eval_jaxpr/psum | solution.py:43
  586.1 0.2 fusion.27
  586.3 55.7 %psum.41 = bf16[64,128]{1,0:T(8,128)(2,1)S(1)} all-reduce(bf16[64,128]{1,0:T(8,128)(2,1)S(1)} %fusion.27), channel_id=1, replica_groups=mesh['row'=16,'col'=16] {'col'}, use_global_device_ids=true, to_apply=%region_3.3 | all-reduce | flops 8192 | bytes 32768 | tf_op jit(solution)/shard_map/while/body/eval_jaxpr/psum | solution.py:11
  641.9 0.1 fusion.28
  642.1 59.6 %psum.40 = bf16[64,128]{1,0:T(8,128)(2,1)S(1)} all-reduce(bf16[64,128]{1,0:T(8,128)(2,1)S(1)} %fusion.26), channel_id=1, replica_groups=mesh['row'=16,'col'=16] {'row'}, use_global_device_ids=true, to_apply=%region_2.2 | all-reduce | flops 8192 | bytes 32768 | tf_op jit(solution)/shard_map/while/body/eval_jaxpr/psum | solution.py:43
  701.7 0.2 fusion.27
  701.9 55.7 %psum.41 = bf16[64,128]{1,0:T(8,128)(2,1)S(1)} all-reduce(bf16[64,128]{1,0:T(8,128)(2,1)S(1)} %fusion.27), channel_id=1, replica_groups=mesh['row'=16,'col'=16] {'col'}, use_global_device_ids=true, to_apply=%region_3.3 | all-reduce | flops 8192 | bytes 32768 | tf_op jit(solution)/shard_map/while/body/eval_jaxpr/psum | solution.py:11
  757.6 0.1 fusion.28
  757.7 59.6 %psum.40 = bf16[64,128]{1,0:T(8,128)(2,1)S(1)} all-reduce(bf16[64,128]{1,0:T(8,128)(2,1)S(1)} %fusion.26), channel_id=1, replica_groups=mesh['row'=16,'col'=16] {'row'}, use_global_device_ids=true, to_apply=%region_2.2 | all-reduce | flops 8192 | bytes 32768 | tf_op jit(solution)/shard_map/while/body/eval_jaxpr/psum | solution.py:43
  817.3 0.2 fusion.27
  817.5 55.7 %psum.41 = bf16[64,128]{1,0:T(8,128)(2,1)S(1)} all-reduce(bf16[64,128]{1,0:T(8,128)(2,1)S(1)} %fusion.27), channel_id=1, replica_groups=mesh['row'=16,'col'=16] {'col'}, use_global_device_ids=true, to_apply=%region_3.3 | all-reduce | flops 8192 | bytes 32768 | tf_op jit(solution)/shard_map/while/body/eval_jaxpr/psum | solution.py:11
  873.2 0.1 fusion.28
  873.3 59.6 %psum.40 = bf16[64,128]{1,0:T(8,128)(2,1)S(1)} all-reduce(bf16[64,128]{1,0:T(8,128)(2,1)S(1)} %fusion.26), channel_id=1, replica_groups=mesh['row'=16,'col'=16] {'row'}, use_global_device_ids=true, to_apply=%region_2.2 | all-reduce | flops 8192 | bytes 32768 | tf_op jit(solution)/shard_map/while/body/eval_jaxpr/psum | solution.py:43
  932.9 0.2 fusion.27
  933.1 55.7 %psum.41 = bf16[64,128]{1,0:T(8,128)(2,1)S(1)} all-reduce(bf16[64,128]{1,0:T(8,128)(2,1)S(1)} %fusion.27), channel_id=1, replica_groups=mesh['row'=16,'col'=16] {'col'}, use_global_device_ids=true, to_apply=%region_3.3 | all-reduce | flops 8192 | bytes 32768 | tf_op jit(solution)/shard_map/while/body/eval_jaxpr/psum | solution.py:11
  988.8 0.1 fusion.28
  988.9 59.6 %psum.40 = bf16[64,128]{1,0:T(8,128)(2,1)S(1)} all-reduce(bf16[64,128]{1,0:T(8,128)(2,1)S(1)} %fusion.26), channel_id=1, replica_groups=mesh['row'=16,'col'=16] {'row'}, use_global_device_ids=true, to_apply=%region_2.2 | all-reduce | flops 8192 | bytes 32768 | tf_op jit(solution)/shard_map/while/body/eval_jaxpr/psum | solution.py:43
  1048.5 0.2 fusion.27
  1048.7 55.7 %psum.41 = bf16[64,128]{1,0:T(8,128)(2,1)S(1)} all-reduce(bf16[64,128]{1,0:T(8,128)(2,1)S(1)} %fusion.27), channel_id=1, replica_groups=mesh['row'=16,'col'=16] {'col'}, use_global_device_ids=true, to_apply=%region_3.3 | all-reduce | flops 8192 | bytes 32768 | tf_op jit(solution)/shard_map/while/body/eval_jaxpr/psum | solution.py:11
  1104.6 59.6 %psum.40 = bf16[64,128]{1,0:T(8,128)(2,1)S(1)} all-reduce(bf16[64,128]{1,0:T(8,128)(2,1)S(1)} %fusion.26), channel_id=1, replica_groups=mesh['row'=16,'col'=16] {'row'}, use_global_device_ids=true, to_apply=%region_2.2 | all-reduce | flops 8192 | bytes 32768 | tf_op jit(solution)/shard_map/while/body/eval_jaxpr/psum | solution.py:43
  1164.2 0.2 fusion.27
  1164.3 55.7 %psum.41 = bf16[64,128]{1,0:T(8,128)(2,1)S(1)} all-reduce(bf16[64,128]{1,0:T(8,128)(2,1)S(1)} %fusion.27), channel_id=1, replica_groups=mesh['row'=16,'col'=16] {'col'}, use_global_device_ids=true, to_apply=%region_3.3 | all-reduce | flops 8192 | bytes 32768 | tf_op jit(solution)/shard_map/while/body/eval_jaxpr/psum | solution.py:11
  1220.0 0.1 fusion.28
  1220.2 59.6 %psum.40 = bf16[64,128]{1,0:T(8,128)(2,1)S(1)} all-reduce(bf16[64,128]{1,0:T(8,128)(2,1)S(1)} %fusion.26), channel_id=1, replica_groups=mesh['row'=16,'col'=16] {'row'}, use_global_device_ids=true, to_apply=%region_2.2 | all-reduce | flops 8192 | bytes 32768 | tf_op jit(solution)/shard_map/while/body/eval_jaxpr/psum | solution.py:43
  1279.8 0.2 fusion.27
  1280.0 55.7 %psum.41 = bf16[64,128]{1,0:T(8,128)(2,1)S(1)} all-reduce(bf16[64,128]{1,0:T(8,128)(2,1)S(1)} %fusion.27), channel_id=1, replica_groups=mesh['row'=16,'col'=16] {'col'}, use_global_device_ids=true, to_apply=%region_3.3 | all-reduce | flops 8192 | bytes 32768 | tf_op jit(solution)/shard_map/while/body/eval_jaxpr/psum | solution.py:11
  1335.7 0.1 fusion.28
  1335.8 59.6 %psum.40 = bf16[64,128]{1,0:T(8,128)(2,1)S(1)} all-reduce(bf16[64,128]{1,0:T(8,128)(2,1)S(1)} %fusion.26), channel_id=1, replica_groups=mesh['row'=16,'col'=16] {'row'}, use_global_device_ids=true, to_apply=%region_2.2 | all-reduce | flops 8192 | bytes 32768 | tf_op jit(solution)/shard_map/while/body/eval_jaxpr/psum | solution.py:43
  1395.4 0.2 fusion.27
  1395.6 55.7 %psum.41 = bf16[64,128]{1,0:T(8,128)(2,1)S(1)} all-reduce(bf16[64,128]{1,0:T(8,128)(2,1)S(1)} %fusion.27), channel_id=1, replica_groups=mesh['row'=16,'col'=16] {'col'}, use_global_device_ids=true, to_apply=%region_3.3 | all-reduce | flops 8192 | bytes 32768 | tf_op jit(solution)/shard_map/while/body/eval_jaxpr/psum | solution.py:11
  1451.4 59.6 %psum.40 = bf16[64,128]{1,0:T(8,128)(2,1)S(1)} all-reduce(bf16[64,128]{1,0:T(8,128)(2,1)S(1)} %fusion.26), channel_id=1, replica_groups=mesh['row'=16,'col'=16] {'row'}, use_global_device_ids=true, to_apply=%region_2.2 | all-reduce | flops 8192 | bytes 32768 | tf_op jit(solution)/shard_map/while/body/eval_jaxpr/psum | solution.py:43
  1511.0 0.2 fusion.27
  1511.2 55.7 %psum.41 = bf16[64,128]{1,0:T(8,128)(2,1)S(1)} all-reduce(bf16[64,128]{1,0:T(8,128)(2,1)S(1)} %fusion.27), channel_id=1, replica_groups=mesh['row'=16,'col'=16] {'col'}, use_global_device_ids=true, to_apply=%region_3.3 | all-reduce | flops 8192 | bytes 32768 | tf_op jit(solution)/shard_map/while/body/eval_jaxpr/psum | solution.py:11
  1567.0 59.6 %psum.40 = bf16[64,128]{1,0:T(8,128)(2,1)S(1)} all-reduce(bf16[64,128]{1,0:T(8,128)(2,1)S(1)} %fusion.26), channel_id=1, replica_groups=mesh['row'=16,'col'=16] {'row'}, use_global_device_ids=true, to_apply=%region_2.2 | all-reduce | flops 8192 | bytes 32768 | tf_op jit(solution)/shard_map/while/body/eval_jaxpr/psum | solution.py:43
  1626.6 0.2 fusion.27
  1626.8 55.7 %psum.41 = bf16[64,128]{1,0:T(8,128)(2,1)S(1)} all-reduce(bf16[64,128]{1,0:T(8,128)(2,1)S(1)} %fusion.27), channel_id=1, replica_groups=mesh['row'=16,'col'=16] {'col'}, use_global_device_ids=true, to_apply=%region_3.3 | all-reduce | flops 8192 | bytes 32768 | tf_op jit(solution)/shard_map/while/body/eval_jaxpr/psum | solution.py:11
  1682.7 59.6 %psum.40 = bf16[64,128]{1,0:T(8,128)(2,1)S(1)} all-reduce(bf16[64,128]{1,0:T(8,128)(2,1)S(1)} %fusion.26), channel_id=1, replica_groups=mesh['row'=16,'col'=16] {'row'}, use_global_device_ids=true, to_apply=%region_2.2 | all-reduce | flops 8192 | bytes 32768 | tf_op jit(solution)/shard_map/while/body/eval_jaxpr/psum | solution.py:43
  1742.3 0.2 fusion.27
  1742.4 55.7 %psum.41 = bf16[64,128]{1,0:T(8,128)(2,1)S(1)} all-reduce(bf16[64,128]{1,0:T(8,128)(2,1)S(1)} %fusion.27), channel_id=1, replica_groups=mesh['row'=16,'col'=16] {'col'}, use_global_device_ids=true, to_apply=%region_3.3 | all-reduce | flops 8192 | bytes 32768 | tf_op jit(solution)/shard_map/while/body/eval_jaxpr/psum | solution.py:11
  1798.3 59.6 %psum.40 = bf16[64,128]{1,0:T(8,128)(2,1)S(1)} all-reduce(bf16[64,128]{1,0:T(8,128)(2,1)S(1)} %fusion.26), channel_id=1, replica_groups=mesh['row'=16,'col'=16] {'row'}, use_global_device_ids=true, to_apply=%region_2.2 | all-reduce | flops 8192 | bytes 32768 | tf_op jit(solution)/shard_map/while/body/eval_jaxpr/psum | solution.py:43
  1857.9 0.2 fusion.27
  1858.1 55.7 %psum.41 = bf16[64,128]{1,0:T(8,128)(2,1)S(1)} all-reduce(bf16[64,128]{1,0:T(8,128)(2,1)S(1)} %fusion.27), channel_id=1, replica_groups=mesh['row'=16,'col'=16] {'col'}, use_global_device_ids=true, to_apply=%region_3.3 | all-reduce | flops 8192 | bytes 32768 | tf_op jit(solution)/shard_map/while/body/eval_jaxpr/psum | solution.py:11
  1913.9 0.6 dynamic-slice_select_fusion
  (54 shorter events, 1.3 us)
Async XLA Ops:
  0.0 22.5 %copy-start = (bf16[64,1,128,128]{3,2,1,0:T(8,128)(2,1)S(1)}, bf16[64,1,128,128]{3,2,1,0:T(8,128)(2,1)}, u32[]{:S(2)}) copy-start(bf16[64,1,128,128]{3,2,1,0:T(8,128)(2,1)} %param.11) | copy-start | bytes 6291460
  0.0 22.4 %copy-start.4 = (s32[64]{0:T(128)S(1)}, s32[64]{0:T(128)}, u32[]{:S(2)}) copy-start(s32[64]{0:T(128)} %param.13) | copy-start | bytes 772
  22.4 52.8 %copy-start.3 = (f32[1,64,128]{2,1,0:T(8,128)S(1)}, f32[1,64,128]{2,1,0:T(8,128)}, u32[]{:S(2)}) copy-start(f32[1,64,128]{2,1,0:T(8,128)} %param.8) | copy-start | bytes 98308
  22.4 52.8 %copy-start.1 = (f32[1,128,128]{2,1,0:T(8,128)S(1)}, f32[1,128,128]{2,1,0:T(8,128)}, u32[]{:S(2)}) copy-start(f32[1,128,128]{2,1,0:T(8,128)} %param.9) | copy-start | bytes 196612
  22.4 52.8 %copy-start.2 = (bf16[1,1,128,128]{3,2,1,0:T(8,128)(2,1)S(1)}, bf16[1,1,128,128]{3,2,1,0:T(8,128)(2,1)}, u32[]{:S(2)}) copy-start(bf16[1,1,128,128]{3,2,1,0:T(8,128)(2,1)} %param.10) | copy-start | bytes 98308
where the time goes:
time: 1930 us; the launch traced here: 1910 us
  blocking collectives  1900 us (98%)
    psum x16, blocking collectives, step_reduced(): lax.psum(partial_value.astype(jnp.bfloat16), 'row').astype(jnp.float32)  940 us
    psum x16, blocking collectives, spread(): return lax.psum(jnp.where(mine, array, jnp.zeros_like(array)), axis)  893 us
    psum x1, blocking collectives, body(): off_sum = lax.psum(off_part, 'row')  50.9 us

commit v1 on v0

v1 whole, which is shorter than its diff:
```python
import functools

import jax
import jax.numpy as jnp
from jax import lax
from jax.experimental import pallas as pl
from jax.experimental.pallas import tpu as pltpu
from jax.sharding import PartitionSpec as P

NB = 16
BS = 128
RHS = 64
TILES = 64
NR = 16
NC = 16
NQ = 8
QR = RHS // NQ
CUT = 11
TRI = NB * (NB - 1) // 2
MESH = pl.DeviceIdType.MESH
BF = jnp.bfloat16
F32 = jnp.float32


def tri(j):
    return j * (j - 1) // 2


def split(value):
    high = value.astype(BF)
    return high, (value - high.astype(F32)).astype(BF)


def kernel(
    rhs_hbm, dinv_hbm, panel_hbm, offdiag_hbm, known_hbm, row_index, out_ref,
    rhs_v, dinv_v, panel_v, off_v, known_v, scaled_v, part_v, pieces_v, panels_v,
    mine_v, pass_v, passed_v, blocks_v,
    load_sem, off_sem, all_in, known_send, known_recv, panel_send, panel_recv,
    part_send, part_recv, pass_send, pass_recv, block_send, block_recv,
):
    r = lax.axis_index("row")
    c = lax.axis_index("col")

    def remote(src, dst, send, recv, row, col):
        return pltpu.make_async_remote_copy(
            src_ref=src, dst_ref=dst, send_sem=send, recv_sem=recv,
            device_id=(row, col), device_id_type=MESH,
        )

    def solver(high, q):
        return 2 * q, jnp.where(high, NC - 4, 0) + q % 4

    barrier = pltpu.get_barrier_semaphore()
    for d in range(1, NC):
        pl.semaphore_signal(barrier, inc=1, device_id=(r, (c + d) % NC), device_id_type=MESH)
    for d in range(1, NR):
        pl.semaphore_signal(barrier, inc=1, device_id=((r + d) % NR, c), device_id_type=MESH)

    mine = pl.ds(2 * c, 2)
    loads = [
        pltpu.make_async_copy(known_hbm, known_v.at[mine], load_sem.at[0]),
        pltpu.make_async_copy(dinv_hbm.at[0], dinv_v, load_sem.at[1]),
        pltpu.make_async_copy(panel_hbm.at[0, 0], panel_v, load_sem.at[2]),
        pltpu.make_async_copy(rhs_hbm.at[0], rhs_v, load_sem.at[3]),
    ]
    for load in loads:
        load.start()
    off_load = pltpu.make_async_copy(offdiag_hbm.at[:, 0], off_v, off_sem)
    off_load.start()
    for load in loads:
        load.wait()

    d_high, d_low = split(dinv_v[...])
    block = panel_v[...]
    scaled = jnp.dot(
        jnp.concatenate([block, block], axis=1),
        jnp.concatenate([d_high, d_low], axis=0),
        preferred_element_type=F32,
    )
    scaled_v[...] = (-scaled).astype(BF)

    pl.semaphore_wait(barrier, NC - 1 + NR - 1)

    for d in (5, 15, 7, 13, 10, 9, 6, 14, 11, 2, 8, 1, 4, 3, 12):
        peer = ((c // 4 + d // 4) % 4) * 4 + (c + d) % 4
        remote(known_v.at[mine], known_v.at[mine], known_send, known_recv, r, peer).start()

    for d in range(1, NR):
        pl.semaphore_signal(all_in, inc=1, device_id=((r + d) % NR, c), device_id_type=MESH)
    pl.semaphore_wait(all_in, NR - 1)

    def panel_copy(q, which):
        row, col = solver(r >= CUT, (r // 2 + q) % NQ)
        spot = tri(r) + c
        if which == "local":
            return pltpu.make_async_copy(scaled_v, panels_v.at[spot], panel_recv.at[r])
        return remote(scaled_v, panels_v.at[spot], panel_send, panel_recv.at[r], row, col)

    own_col = jnp.where(r >= CUT, NC - 4, 0) + (r // 2) % 4
    panel_self = (r % 2 == 0) & (c == own_col)

    @pl.when(c < r)
    def _():
        for q in range(NQ):
            if q == 0:
                pl.when(panel_self)(lambda: panel_copy(0, "local").start())
                pl.when(jnp.logical_not(panel_self))(lambda: panel_copy(0, "remote").start())
            else:
                panel_copy(q, "remote").start()

    rest = pl.ds(0, 2 * (NC - 1))
    remote(known_v.at[rest], known_v.at[rest], known_send, known_recv, r, (c + 1) % NC).wait_recv()
    off_load.wait()
    total = jnp.zeros((RHS, BS), F32)
    for p in range(0, TILES, 2):
        picked = jnp.concatenate([known_v[row_index[p]], known_v[row_index[p + 1]]], axis=1)
        total = total + jnp.dot(
            picked, off_v[p : p + 2].reshape(2 * BS, BS), preferred_element_type=F32
        )
    once = (r == 0).astype(F32)
    t_high, t_low = split(rhs_v[...] * once - total)
    part = jnp.dot(
        jnp.concatenate([t_high, t_high, t_low], axis=1),
        jnp.concatenate([d_high, d_low, d_high], axis=0),
        preferred_element_type=F32,
    )
    part_v[...] = part.astype(BF).reshape(NQ, QR, BS)

    part_col = jnp.where(c >= CUT, NC - 4, 0) + (r // 2) % 4
    part_self = (r % 2 == 0) & (c == part_col)

    def part_copy(q, which):
        group = (r // 2 + q) % NQ
        row, col = solver(c >= CUT, group)
        if which == "local":
            return pltpu.make_async_copy(part_v.at[group], pieces_v.at[c, r], part_recv.at[c])
        return remote(part_v.at[group], pieces_v.at[c, r], part_send, part_recv.at[c], row, col)

    for q in range(NQ):
        if q == 0:
            pl.when(part_self)(lambda: part_copy(0, "local").start())
            pl.when(jnp.logical_not(part_self))(lambda: part_copy(0, "remote").start())
        else:
            part_copy(q, "remote").start()

    my_q = r // 2
    even = r % 2 == 0
    is_high = even & (c == NC - 4 + my_q % 4)
    is_low = even & (c == my_q % 4)

    def block_copy(k, d, which):
        if which == "local":
            return pltpu.make_async_copy(mine_v.at[k], blocks_v.at[my_q], block_recv)
        row = (r + d) % NR
        return remote(mine_v.at[k], blocks_v.at[my_q], block_send.at[k], block_recv, row, k)

    def send_block(k):
        for d in range(NR):
            if d == 0:
                pl.when(c == k)(lambda: block_copy(k, 0, "local").start())
                pl.when(c != k)(lambda: block_copy(k, 0, "remote").start())
            else:
                block_copy(k, d, "remote").start()

    def finish_block(k):
        for d in range(NR):
            if d == 0:
                pl.when(c != k)(lambda: block_copy(k, 0, "remote").wait_send())
            else:
                block_copy(k, d, "remote").wait_send()

    def summed(k):
        pltpu.make_async_copy(pieces_v.at[k], pieces_v.at[k], part_recv.at[k]).wait()
        return jnp.sum(pieces_v[k].astype(F32), axis=0)

    def rows_in(j):
        if j > 0:
            spots = pl.ds(tri(j), j)
            pltpu.make_async_copy(panels_v.at[spots], panels_v.at[spots], panel_recv.at[j]).wait()

    def eliminate(j, sums):
        done = sums[j].astype(BF)
        mine_v[j] = done
        send_block(j)
        for k in range(j - 1, -1, -1):
            term = jnp.dot(done, panels_v[tri(j) + k], preferred_element_type=F32)
            sums[k] = term if sums[k] is None else sums[k] + term

    @pl.when(is_high)
    def _():
        for j in range(NB - 1, CUT - 1, -1):
            rows_in(j)
        sums = [None] * CUT + [summed(k) for k in range(CUT, NB)]
        for j in range(NB - 1, CUT - 1, -1):
            eliminate(j, sums)
        for k in range(CUT):
            pass_v[k] = sums[k]
        remote(pass_v, passed_v, pass_send, pass_recv, r, my_q % 4).start()
        remote(pass_v, passed_v, pass_send, pass_recv, r, my_q % 4).wait_send()
        for k in range(CUT, NB):
            finish_block(k)

    @pl.when(is_low)
    def _():
        for j in range(CUT - 1, -1, -1):
            rows_in(j)
        sums = [summed(k) for k in range(CUT)]
        remote(pass_v, passed_v, pass_send, pass_recv, r, my_q % 4 + NC - 4).wait_recv()
        sums = [sums[k] + passed_v[k] for k in range(CUT)]
        for j in range(CUT - 1, -1, -1):
            eliminate(j, sums)
        for k in range(CUT):
            finish_block(k)

    pltpu.make_async_copy(blocks_v, blocks_v, block_recv).wait()
    out_ref[0] = blocks_v[...].reshape(RHS, BS)

    remote(known_v.at[rest], known_v.at[rest], known_send, known_recv, r, (c + 1) % NC).wait_send()

    @pl.when(c < r)
    def _():
        pl.when(jnp.logical_not(panel_self))(lambda: panel_copy(0, "remote").wait_send())
        for q in range(1, NQ):
            panel_copy(q, "remote").wait_send()

    pl.when(jnp.logical_not(part_self))(lambda: part_copy(0, "remote").wait_send())
    for q in range(1, NQ):
        part_copy(q, "remote").wait_send()


def body(rhs, diag_inv, panel, offdiag, known, row_index):
    anywhere = pl.BlockSpec(memory_space=pl.ANY)
    dma = pltpu.SemaphoreType.DMA
    return pl.pallas_call(
        kernel,
        out_shape=jax.ShapeDtypeStruct((1, RHS, BS), BF),
        in_specs=[anywhere] * 5 + [pl.BlockSpec(memory_space=pltpu.SMEM)],
        out_specs=pl.BlockSpec(memory_space=pltpu.VMEM),
        scratch_shapes=[
            pltpu.VMEM((RHS, BS), F32),
            pltpu.VMEM((BS, BS), F32),
            pltpu.VMEM((BS, BS), BF),
            pltpu.VMEM((TILES, BS, BS), BF),
            pltpu.VMEM((2 * NC, RHS, BS), BF),
            pltpu.VMEM((BS, BS), BF),
            pltpu.VMEM((NQ, QR, BS), BF),
            pltpu.VMEM((NC, NR, QR, BS), BF),
            pltpu.VMEM((TRI, BS, BS), BF),
            pltpu.VMEM((NB, QR, BS), BF),
            pltpu.VMEM((CUT, QR, BS), F32),
            pltpu.VMEM((CUT, QR, BS), F32),
            pltpu.VMEM((NQ, QR, BS), BF),
            dma((4,)),
            dma,
            pltpu.SemaphoreType.REGULAR,
            dma, dma, dma, dma((NR,)), dma, dma((NC,)), dma, dma, dma((NB,)), dma,
        ],
        compiler_params=pltpu.CompilerParams(
            collective_id=0, has_side_effects=True, vmem_limit_bytes=32 << 20
        ),
    )(rhs, diag_inv, panel, offdiag, known, row_index)


def solution(mesh):
    placed = (
        P("col", None, None),
        P("col", None, None),
        P("row", "col", None, None),
        P("row", "col", None, None),
        P(("row", "col"), None, None),
        P("row"),
    )
    return jax.shard_map(
        body, mesh=mesh, in_specs=placed, out_specs=P("col", None, None), check_vma=False
    )
```

time: 1930 us -> 56.2 us (0.03)
  blocking collectives: 1900 us -> 0 us
  Pallas kernels: 0 us -> 49.8 us
    psum x33 -> x0, blocking collectives: 1880 us -> none  [the longest x16 940 us: step_reduced(): lax.psum(partial_value.astype(jnp.bfloat16), 'row').astype(jnp.float32)]
    pallas_call x0 -> x1, Pallas kernels: none -> 49.8 us  [body(): pl.pallas_call(kernel, out_shape=jax.ShapeDtypeStruct((1, RHS, BS), BF),...]
    all_gather x1 -> x0, blocking collectives: 20.1 us -> none  [body(): known_row = lax.all_gather(known, 'col', axis=0, tiled=True)]
where the time goes in v1:
time: 56.2 us; the launch traced here: 55.8 us
  Pallas kernels  49.8 us (89%)
  local copies, waits for them, and re-layouts  5.96 us (11%)
    pallas_call x1, Pallas kernels, body(): pl.pallas_call(kernel, out_shape=jax.ShapeDtypeStruct((1, RHS, BS), BF),...  49.8 us
    unnamed x13, local copies, waits for them, and re-layouts  5.96 us

profile of v1, /device:TPU:1, one launch (start us, length us, event | category | flops | bytes accessed | tf_op | source)
XLA Modules:
  0.0 55.8 jit_solution(8437653676035588274)
XLA Ops:
  0.0 0.0 copy-start
  0.0 1.6 %copy-done = bf16[64,1,128,128]{3,2,1,0:T(8,128)(2,1)S(1)} copy-done((bf16[64,1,128,128]{3,2,1,0:T(8,128)(2,1)S(1)}, bf16[64,1,128,128]{3,2,1,0:T(8,128)(2,1)}, u32[]{:S(2)}) %copy-start) | copy-done | bytes 2097176
  1.6 0.0 copy-start.1
  1.6 0.8 %copy-done.1 = f32[1,128,128]{2,1,0:T(8,128)S(1)} copy-done((f32[1,128,128]{2,1,0:T(8,128)S(1)}, f32[1,128,128]{2,1,0:T(8,128)}, u32[]{:S(2)}) %copy-start.1) | copy-done | bytes 65560
  2.4 0.0 copy-start.2
  2.4 0.8 %copy-done.2 = f32[1,64,128]{2,1,0:T(8,128)S(1)} copy-done((f32[1,64,128]{2,1,0:T(8,128)S(1)}, f32[1,64,128]{2,1,0:T(8,128)}, u32[]{:S(2)}) %copy-start.2) | copy-done | bytes 32792
  3.2 0.0 copy-start.3
  3.2 0.8 %copy-done.3 = bf16[1,1,128,128]{3,2,1,0:T(8,128)(2,1)S(1)} copy-done((bf16[1,1,128,128]{3,2,1,0:T(8,128)(2,1)S(1)}, bf16[1,1,128,128]{3,2,1,0:T(8,128)(2,1)}, u32[]{:S(2)}) %copy-start.3) | copy-done | bytes 32792
  3.9 0.0 copy-start.4
  4.0 0.8 %copy-done.4 = bf16[2,64,128]{2,1,0:T(8,128)(2,1)S(1)} copy-done((bf16[2,64,128]{2,1,0:T(8,128)(2,1)S(1)}, bf16[2,64,128]{2,1,0:T(8,128)(2,1)}, u32[]{:S(2)}) %copy-start.4) | copy-done | bytes 32792
  4.7 0.0 copy-start.5
  4.7 0.7 %copy-done.5 = s32[64]{0:T(128)S(1)} copy-done((s32[64]{0:T(128)S(1)}, s32[64]{0:T(128)}, u32[]{:S(2)}) %copy-start.5) | copy-done | bytes 280
  5.4 49.8 %shard_map.64 = bf16[1,64,128]{2,1,0:T(8,128)(2,1)S(1)} custom-call(f32[1,64,128]{2,1,0:T(8,128)S(1)} %copy-done.2, f32[1,128,128]{2,1,0:T(8,128)S(1)} %copy-done.1, bf16[1,1,128,128]{3,2,1,0:T(8,128)(2,1)S(1)} %copy-done.3, bf16[64,1,128,128]{3,2,1,0:T(8,128)(2,1)S(1)} %copy-done, bf16[2,64,128]{2,1,0:T(8,128)(2,1)S(1)} %copy-done.4, s32[64]{0:T(128)S(1)} %copy-done.5), custom_call_target="tpu_custom_call" | custom-call | tf_op jit(solution)/shard_map/pallas_call | solution.py:234
  55.2 0.6 %copy.8 = bf16[1,64,128]{2,1,0:T(8,128)(2,1)} copy(bf16[1,64,128]{2,1,0:T(8,128)(2,1)S(1)} %shard_map.64) | data formatting | bytes 32768
Async XLA Ops:
  0.0 1.6 %copy-start = (bf16[64,1,128,128]{3,2,1,0:T(8,128)(2,1)S(1)}, bf16[64,1,128,128]{3,2,1,0:T(8,128)(2,1)}, u32[]{:S(2)}) copy-start(bf16[64,1,128,128]{3,2,1,0:T(8,128)(2,1)} %offdiag_hbm.1) | copy-start | bytes 6291460
  1.6 0.8 %copy-start.1 = (f32[1,128,128]{2,1,0:T(8,128)S(1)}, f32[1,128,128]{2,1,0:T(8,128)}, u32[]{:S(2)}) copy-start(f32[1,128,128]{2,1,0:T(8,128)} %dinv_hbm.1) | copy-start | bytes 196612
  2.4 0.8 %copy-start.2 = (f32[1,64,128]{2,1,0:T(8,128)S(1)}, f32[1,64,128]{2,1,0:T(8,128)}, u32[]{:S(2)}) copy-start(f32[1,64,128]{2,1,0:T(8,128)} %rhs_hbm.1) | copy-start | bytes 98308
  3.2 0.8 %copy-start.3 = (bf16[1,1,128,128]{3,2,1,0:T(8,128)(2,1)S(1)}, bf16[1,1,128,128]{3,2,1,0:T(8,128)(2,1)}, u32[]{:S(2)}) copy-start(bf16[1,1,128,128]{3,2,1,0:T(8,128)(2,1)} %panel_hbm.1) | copy-start | bytes 98308
  3.9 0.8 %copy-start.4 = (bf16[2,64,128]{2,1,0:T(8,128)(2,1)S(1)}, bf16[2,64,128]{2,1,0:T(8,128)(2,1)}, u32[]{:S(2)}) copy-start(bf16[2,64,128]{2,1,0:T(8,128)(2,1)} %known_hbm.1) | copy-start | bytes 98308
  4.7 0.7 %copy-start.5 = (s32[64]{0:T(128)S(1)}, s32[64]{0:T(128)}, u32[]{:S(2)}) copy-start(s32[64]{0:T(128)} %row_index.1) | copy-start | bytes 772

commit v2 on v1

v2 whole, which is shorter than its diff:
```python
import jax
import jax.numpy as jnp
from jax import lax
from jax.experimental import pallas as pl
from jax.experimental.pallas import tpu as pltpu
from jax.sharding import PartitionSpec as P

NB = 16
BS = 128
RHS = 64
TILES = 64
NR = 16
NC = 16
NQ = 4
QR = RHS // NQ
CUT = 11
TOP = NB - CUT
SIDE = 4
MESH = pl.DeviceIdType.MESH
BF = jnp.bfloat16
F32 = jnp.float32
SPOT_Z = (0, 1, 2, 3)
HIGH_X = (3, 2) * 4
LOW_X = (0, 1) * 4


def tri(j):
    return j * (j - 1) // 2


def spot(j, k):
    d = k - CUT
    return d * (TOP - 1) - d * (d - 1) // 2 + j - k - 1


def split(value):
    high = value.astype(BF)
    return high, (value - high.astype(F32)).astype(BF)


def kernel(
    rhs_hbm, dinv_hbm, panel_hbm, offdiag_hbm, known_hbm, row_index, out_ref,
    rhs_v, dinv_v, panel_v, off_v, known_v, scaled_v, part_v, pieces_v,
    top_v, cross_v, low_v, mine_v, pass_v, passed_v, blocks_v,
    load_sem, off_sem, planes_in, all_in, known_send, known_recv,
    panel_send, top_recv, cross_recv, low_recv, share_send, share_recv,
    part_send, part_recv, pass_send, pass_recv, block_send, block_recv,
):
    r = lax.axis_index("row")
    c = lax.axis_index("col")
    y = c % SIDE

    def signal(sem, row, col):
        pl.semaphore_signal(sem, inc=1, device_id=(row, col), device_id_type=MESH)

    def remote(src, dst, send, recv, row, col):
        return pltpu.make_async_remote_copy(
            src_ref=src, dst_ref=dst, send_sem=send, recv_sem=recv,
            device_id=(row, col), device_id_type=MESH,
        )

    def start_to(place, src, dst, send, recv):
        here = (r == place[0]) & (c == place[1])
        pl.when(here)(lambda: pltpu.make_async_copy(src, dst, recv).start())
        pl.when(jnp.logical_not(here))(lambda: remote(src, dst, send, recv, *place).start())

    def finish_to(place, src, send, recv):
        here = (r == place[0]) & (c == place[1])
        pl.when(jnp.logical_not(here))(lambda: remote(src, src, send, recv, *place).wait_send())

    def arrived(dst, sem):
        pltpu.make_async_copy(dst, dst, sem).wait()

    def high_at(q, i):
        return 2 * SPOT_Z[q], HIGH_X[q] * SIDE + i

    def low_at(q):
        return 2 * SPOT_Z[q], LOW_X[q] * SIDE

    barrier = pltpu.get_barrier_semaphore()
    for d in range(1, NC):
        signal(barrier, r, (c + d) % NC)

    @pl.when(c == 0)
    def _():
        for d in range(1, NR):
            signal(barrier, (r + d) % NR, 0)

    mine = pl.ds(2 * c, 2)
    known_load = pltpu.make_async_copy(known_hbm, known_v.at[mine], load_sem.at[0])
    loads = [
        pltpu.make_async_copy(dinv_hbm.at[0], dinv_v, load_sem.at[1]),
        pltpu.make_async_copy(panel_hbm.at[0, 0], panel_v, load_sem.at[2]),
        pltpu.make_async_copy(rhs_hbm.at[0], rhs_v, load_sem.at[3]),
    ]
    known_load.start()
    for load in loads:
        load.start()
    off_load = pltpu.make_async_copy(offdiag_hbm.at[:, 0], off_v, off_sem)
    off_load.start()
    known_load.wait()
    pl.when(c == 0)(lambda: pl.semaphore_wait(barrier, NC - 1 + NR - 1))
    pl.when(c != 0)(lambda: pl.semaphore_wait(barrier, NC - 1))

    for d in (5, 15, 7, 13, 10, 9, 6, 14, 11, 2, 8, 1, 4, 3, 12):
        peer = ((c // SIDE + d // SIDE) % SIDE) * SIDE + (c + d) % SIDE
        remote(known_v.at[mine], known_v.at[mine], known_send, known_recv, r, peer).start()

    @pl.when(c == 0)
    def _():
        for d in range(1, NR):
            signal(planes_in, (r + d) % NR, 0)

    for load in loads:
        load.wait()
    d_high, d_low = split(dinv_v[...])
    block = panel_v[...]
    scaled = jnp.dot(
        jnp.concatenate([block, block], axis=1),
        jnp.concatenate([d_high, d_low], axis=0),
        preferred_element_type=F32,
    )
    scaled_v[...] = (-scaled).astype(BF)

    @pl.when(c == 0)
    def _():
        pl.semaphore_wait(planes_in, NR - 1)
        for d in range(1, NC):
            signal(all_in, r, (c + d) % NC)

    @pl.when(c != 0)
    def _():
        pl.semaphore_wait(all_in, 1)

    in_top = (r >= CUT) & (c >= CUT) & (c < r)
    in_cross = (r >= CUT) & (c < CUT)
    in_low = (r < CUT) & (c < r)

    @pl.when(in_top)
    def _():
        for q in range(NQ):
            start_to(high_at(q, y), scaled_v, top_v.at[spot(r, c)], panel_send, top_recv)

    @pl.when(in_cross)
    def _():
        for q in range(NQ):
            start_to(high_at(q, y), scaled_v, cross_v.at[c // SIDE, NB - 1 - r], panel_send, cross_recv)

    @pl.when(in_low)
    def _():
        for q in range(NQ):
            start_to(low_at(q), scaled_v, low_v.at[tri(r) + c], panel_send, low_recv)

    rest = pl.ds(0, 2 * (NC - 1))
    arrived(known_v.at[rest], known_recv)
    off_load.wait()
    total = jnp.zeros((RHS, BS), F32)
    for p in range(0, TILES, 2):
        picked = jnp.concatenate([known_v[row_index[p]], known_v[row_index[p + 1]]], axis=1)
        total = total + jnp.dot(
            picked, off_v[p : p + 2].reshape(2 * BS, BS), preferred_element_type=F32
        )
    once = (r == 0).astype(F32)
    t_high, t_low = split(rhs_v[...] * once - total)
    part = jnp.dot(
        jnp.concatenate([t_high, t_high, t_low], axis=1),
        jnp.concatenate([d_high, d_low, d_high], axis=0),
        preferred_element_type=F32,
    )
    part_v[...] = part.astype(BF).reshape(NQ, QR, BS)

    @pl.when(c >= CUT)
    def _():
        for q in range(NQ):
            for i in range(SIDE):
                start_to(high_at(q, i), part_v.at[q], pieces_v.at[c, r], part_send, part_recv)

    @pl.when(c < CUT)
    def _():
        for q in range(NQ):
            start_to(low_at(q), part_v.at[q], pieces_v.at[c, r], part_send, part_recv)

    def block_copy(k, d, my_q):
        return remote(
            mine_v.at[k], blocks_v.at[my_q], block_send.at[k], block_recv, (r + d) % NR, k
        )

    def send_block(k, my_q, may_be_own):
        for d in range(NR):
            if d == 0 and may_be_own:
                own = pltpu.make_async_copy(mine_v.at[k], blocks_v.at[my_q], block_recv)
                pl.when(c == k)(lambda: own.start())
                pl.when(c != k)(lambda: block_copy(k, 0, my_q).start())
            else:
                block_copy(k, d, my_q).start()

    def finish_block(k, my_q, may_be_own):
        for d in range(NR):
            if d == 0 and may_be_own:
                pl.when(c != k)(lambda: block_copy(k, 0, my_q).wait_send())
            else:
                block_copy(k, d, my_q).wait_send()

    def member(places):
        one, which = jnp.bool_(False), jnp.int32(0)
        for q, options in enumerate(places):
            here = jnp.bool_(False)
            for row, col in options:
                here = here | ((r == row) & (c == col))
            one, which = one | here, which + jnp.where(here, q, 0)
        return one, which

    is_high, high_q = member([[high_at(q, i) for i in range(SIDE)] for q in range(NQ)])
    is_low, low_q = member([[low_at(q)] for q in range(NQ)])

    def summed(k):
        return jnp.sum(pieces_v[k].astype(F32), axis=0)

    @pl.when(is_high)
    def _():
        for k in range(CUT, NB - 1):
            count = NB - 1 - k
            column = top_v.at[pl.ds(spot(k + 1, k), count)]
            others = top_v.at[pl.ds(0, tri(TOP) - count)]

            def to(d):
                return remote(column, column, share_send, share_recv, r, c - y + (y + d) % SIDE)

            @pl.when(y == k % SIDE)
            def _():
                arrived(column, top_recv)
                for d in range(1, SIDE):
                    to(d).start()
                arrived(others, share_recv)
                for d in range(1, SIDE):
                    to(d).wait_send()

        pl.when(y < CUT - 2 * SIDE)(lambda: arrived(cross_v, cross_recv))
        pl.when(y >= CUT - 2 * SIDE)(lambda: arrived(cross_v.at[pl.ds(0, 2)], cross_recv))
        arrived(pieces_v.at[pl.ds(CUT, TOP)], part_recv)
        sums = [summed(k) for k in range(CUT, NB)]
        done = [None] * TOP
        for j in range(TOP - 1, -1, -1):
            done[j] = sums[j].astype(BF)
            mine_v[CUT + j] = done[j]
            for k in range(j - 1, -1, -1):
                sums[k] += jnp.dot(done[j], top_v[spot(CUT + j, CUT + k)], preferred_element_type=F32)
        joined = jnp.concatenate(done[::-1], axis=1)
        low_col = (SIDE - 1 - c // SIDE) * SIDE

        def cross(t):
            return remote(
                pass_v.at[t], passed_v.at[t * SIDE + y], pass_send, pass_recv, r, low_col
            )

        def send_cross(t):
            pass_v[t] = jnp.dot(
                joined, cross_v[t].reshape(TOP * BS, BS), preferred_element_type=F32
            )
            cross(t).start()

        @pl.when(y < CUT - 2 * SIDE)
        def _():
            send_cross(2)

        send_cross(1)
        send_cross(0)
        for k in range(CUT, NB):
            pl.when(y == k % SIDE)(lambda: send_block(k, high_q, True))
        cross(0).wait_send()
        cross(1).wait_send()
        pl.when(y < CUT - 2 * SIDE)(lambda: cross(2).wait_send())
        for k in range(CUT, NB):
            pl.when(y == k % SIDE)(lambda: finish_block(k, high_q, True))

    @pl.when(is_low)
    def _():
        arrived(low_v, low_recv)
        arrived(pieces_v.at[pl.ds(0, CUT)], part_recv)
        sums = [summed(k) for k in range(CUT)]
        arrived(passed_v, pass_recv)
        sums = [sums[k] + passed_v[k] for k in range(CUT)]
        for j in range(CUT - 1, -1, -1):
            done = sums[j].astype(BF)
            mine_v[j] = done
            send_block(j, low_q, j in (0, SIDE))
            for k in range(j - 1, -1, -1):
                sums[k] += jnp.dot(done, low_v[tri(j) + k], preferred_element_type=F32)
        for k in range(CUT):
            finish_block(k, low_q, k in (0, SIDE))

    arrived(blocks_v, block_recv)
    out_ref[0] = blocks_v[...].reshape(RHS, BS)

    remote(known_v.at[rest], known_v.at[rest], known_send, known_recv, r, (c + 1) % NC).wait_send()

    @pl.when(in_top)
    def _():
        for q in range(NQ):
            finish_to(high_at(q, y), scaled_v, panel_send, top_recv)

    @pl.when(in_cross)
    def _():
        for q in range(NQ):
            finish_to(high_at(q, y), scaled_v, panel_send, cross_recv)

    @pl.when(in_low)
    def _():
        for q in range(NQ):
            finish_to(low_at(q), scaled_v, panel_send, low_recv)

    @pl.when(c >= CUT)
    def _():
        for q in range(NQ):
            for i in range(SIDE):
                finish_to(high_at(q, i), part_v.at[q], part_send, part_recv)

    @pl.when(c < CUT)
    def _():
        for q in range(NQ):
            finish_to(low_at(q), part_v.at[q], part_send, part_recv)


def body(rhs, diag_inv, panel, offdiag, known, row_index):
    anywhere = pl.BlockSpec(memory_space=pl.ANY)
    dma = pltpu.SemaphoreType.DMA
    regular = pltpu.SemaphoreType.REGULAR
    return pl.pallas_call(
        kernel,
        out_shape=jax.ShapeDtypeStruct((1, RHS, BS), BF),
        in_specs=[anywhere] * 5 + [pl.BlockSpec(memory_space=pltpu.SMEM)],
        out_specs=pl.BlockSpec(memory_space=pltpu.VMEM),
        scratch_shapes=[
            pltpu.VMEM((RHS, BS), F32),
            pltpu.VMEM((BS, BS), F32),
            pltpu.VMEM((BS, BS), BF),
            pltpu.VMEM((TILES, BS, BS), BF),
            pltpu.VMEM((2 * NC, RHS, BS), BF),
            pltpu.VMEM((BS, BS), BF),
            pltpu.VMEM((NQ, QR, BS), BF),
            pltpu.VMEM((NC, NR, QR, BS), BF),
            pltpu.VMEM((tri(TOP), BS, BS), BF),
            pltpu.VMEM((3, TOP, BS, BS), BF),
            pltpu.VMEM((tri(CUT), BS, BS), BF),
            pltpu.VMEM((NB, QR, BS), BF),
            pltpu.VMEM((3, QR, BS), F32),
            pltpu.VMEM((CUT, QR, BS), F32),
            pltpu.VMEM((NQ, QR, BS), BF),
            dma((4,)), dma, regular, regular, dma, dma,
            dma, dma, dma, dma, dma, dma,
            dma, dma, dma, dma, dma((NB,)), dma,
        ],
        compiler_params=pltpu.CompilerParams(collective_id=0, has_side_effects=True),
    )(rhs, diag_inv, panel, offdiag, known, row_index)


def solution(mesh):
    placed = (
        P("col", None, None),
        P("col", None, None),
        P("row", "col", None, None),
        P("row", "col", None, None),
        P(("row", "col"), None, None),
        P("row"),
    )
    return jax.shard_map(
        body, mesh=mesh, in_specs=placed, out_specs=P("col", None, None), check_vma=False
    )
```

time: 56.2 us -> 44.7 us (0.80)
  Pallas kernels: 49.8 us -> 43.1 us
  local copies, waits for them, and re-layouts: 5.96 us -> 1.32 us
    pallas_call x1, Pallas kernels: 49.8 us -> 43.1 us  [body(): pl.pallas_call(kernel, out_shape=jax.ShapeDtypeStruct((1, RHS, BS), BF),...]
    unnamed x13 -> x1, local copies, waits for them, and re-layouts: 5.96 us -> 1.32 us
where the time goes in v2:
time: 44.7 us; the launch traced here: 44.5 us
  Pallas kernels  43.1 us (96%)
  local copies, waits for them, and re-layouts  1.32 us (3%)
    pallas_call x1, Pallas kernels, body(): pl.pallas_call(kernel, out_shape=jax.ShapeDtypeStruct((1, RHS, BS), BF),...  43.1 us
    unnamed x1, local copies, waits for them, and re-layouts  1.32 us

profile of v2, /device:TPU:1, one launch (start us, length us, event | category | flops | bytes accessed | tf_op | source)
XLA Modules:
  0.0 44.5 jit_solution(13779160148038189102)
XLA Ops:
  0.0 43.1 %shard_map.64 = bf16[1,64,128]{2,1,0:T(8,128)(2,1)} custom-call(f32[1,64,128]{2,1,0:T(8,128)} %rhs_hbm.1, f32[1,128,128]{2,1,0:T(8,128)} %dinv_hbm.1, bf16[1,1,128,128]{3,2,1,0:T(8,128)(2,1)} %panel_hbm.1, bf16[64,1,128,128]{3,2,1,0:T(8,128)(2,1)} %offdiag_hbm.1, bf16[2,64,128]{2,1,0:T(8,128)(2,1)} %known_hbm.1, s32[64]{0:T(128)} %row_index.1), custom_call_target="tpu_custom_call" | custom-call | tf_op jit(solution)/shard_map/pallas_call | solution.py:328
  43.2 1.3 %copy.8 = bf16[1,64,128]{2,1,0:T(8,128)(2,1)} copy(bf16[1,64,128]{2,1,0:T(8,128)(2,1)} %shard_map.64) | data formatting | bytes 32768

commit v3 on v2

--- a/solution.py
+++ b/solution.py
@@ -13,6 +13,9 @@
 NC = 16
 NQ = 4
 QR = RHS // NQ
+NL = 8
+LR = RHS // NL
+PER = NL // NQ
 CUT = 11
 TOP = NB - CUT
 SIDE = 4
@@ -20,8 +23,8 @@
 BF = jnp.bfloat16
 F32 = jnp.float32
 SPOT_Z = (0, 1, 2, 3)
-HIGH_X = (3, 2) * 4
-LOW_X = (0, 1) * 4
+HIGH_X = (3, 3, 3, 3)
+LOW_X = (0, 1)
 
 
 def tri(j):
@@ -40,8 +43,9 @@
 
 def kernel(
     rhs_hbm, dinv_hbm, panel_hbm, offdiag_hbm, known_hbm, row_index, out_ref,
-    rhs_v, dinv_v, panel_v, off_v, known_v, scaled_v, part_v, pieces_v,
-    top_v, cross_v, low_v, mine_v, pass_v, passed_v, blocks_v,
+    rhs_v, dinv_v, panel_v, off_v, known_v, scaled_v,
+    high_part_v, low_part_v, high_pieces_v, low_pieces_v, top_v, cross_v, low_v,
+    high_mine_v, low_mine_v, pass_v, passed_v, high_blocks_v, low_blocks_v,
     load_sem, off_sem, planes_in, all_in, known_send, known_recv,
     panel_send, top_recv, cross_recv, low_recv, share_send, share_recv,
     part_send, part_recv, pass_send, pass_recv, block_send, block_recv,
@@ -74,8 +78,20 @@
     def high_at(q, i):
         return 2 * SPOT_Z[q], HIGH_X[q] * SIDE + i
 
-    def low_at(q):
-        return 2 * SPOT_Z[q], LOW_X[q] * SIDE
+    def low_at(g):
+        return 2 * SPOT_Z[g // PER], LOW_X[g % PER] * SIDE
+
+    def member(places):
+        one, which = jnp.bool_(False), jnp.int32(0)
+        for q, options in enumerate(places):
+            here = jnp.bool_(False)
+            for row, col in options:
+                here = here | ((r == row) & (c == col))
+            one, which = one | here, which + jnp.where(here, q, 0)
+        return one, which
+
+    is_high, high_q = member([[high_at(q, i) for i in range(SIDE)] for q in range(NQ)])
+    is_low, low_q = member([[low_at(g)] for g in range(NL)])
 
     barrier = pltpu.get_barrier_semaphore()
     for d in range(1, NC):
@@ -85,6 +101,21 @@
     def _():
         for d in range(1, NR):
             signal(barrier, (r + d) % NR, 0)
+
+    @pl.when(is_high)
+    def _():
+        for j in range(CUT, NB):
+            for t in range(SIDE):
+                pl.when(t * SIDE + y < j)(lambda: signal(barrier, j, t * SIDE + y))
+
+    @pl.when(is_low)
+    def _():
+        for j in range(1, CUT):
+            for k in range(j):
+                if k % SIDE == 0:
+                    pl.when((r != j) | (c != k))(lambda: signal(barrier, j, k))
+                else:
+                    signal(barrier, j, k)
 
     mine = pl.ds(2 * c, 2)
     known_load = pltpu.make_async_copy(known_hbm, known_v.at[mine], load_sem.at[0])
@@ -99,8 +130,8 @@
     off_load = pltpu.make_async_copy(offdiag_hbm.at[:, 0], off_v, off_sem)
     off_load.start()
     known_load.wait()
-    pl.when(c == 0)(lambda: pl.semaphore_wait(barrier, NC - 1 + NR - 1))
-    pl.when(c != 0)(lambda: pl.semaphore_wait(barrier, NC - 1))
+    greeted = NC - 1 + jnp.where(c == 0, NR - 1, 0) + jnp.where(c < r, jnp.where(r < CUT, NL, NQ), 0)
+    pl.semaphore_wait(barrier, greeted - jnp.where(is_low & (c < r), 1, 0))
 
     for d in (5, 15, 7, 13, 10, 9, 6, 14, 11, 2, 8, 1, 4, 3, 12):
         peer = ((c // SIDE + d // SIDE) % SIDE) * SIDE + (c + d) % SIDE
@@ -122,6 +153,25 @@
     )
     scaled_v[...] = (-scaled).astype(BF)
 
+    in_top = (r >= CUT) & (c >= CUT) & (c < r)
+    in_cross = (r >= CUT) & (c < CUT)
+    in_low = (r < CUT) & (c < r)
+
+    @pl.when(in_top)
+    def _():
+        for q in range(NQ):
+            start_to(high_at(q, y), scaled_v, top_v.at[spot(r, c)], panel_send, top_recv)
+
+    @pl.when(in_cross)
+    def _():
+        for q in range(NQ):
+            start_to(high_at(q, y), scaled_v, cross_v.at[c // SIDE, NB - 1 - r], panel_send, cross_recv)
+
+    @pl.when(in_low)
+    def _():
+        for q in range(NL):
+            start_to(low_at(q), scaled_v, low_v.at[tri(r) + c], panel_send, low_recv)
+
     @pl.when(c == 0)
     def _():
         pl.semaphore_wait(planes_in, NR - 1)
@@ -131,25 +181,6 @@
     @pl.when(c != 0)
     def _():
         pl.semaphore_wait(all_in, 1)
-
-    in_top = (r >= CUT) & (c >= CUT) & (c < r)
-    in_cross = (r >= CUT) & (c < CUT)
-    in_low = (r < CUT) & (c < r)
-
-    @pl.when(in_top)
-    def _():
-        for q in range(NQ):
-            start_to(high_at(q, y), scaled_v, top_v.at[spot(r, c)], panel_send, top_recv)
-
-    @pl.when(in_cross)
-    def _():
-        for q in range(NQ):
-            start_to(high_at(q, y), scaled_v, cross_v.at[c // SIDE, NB - 1 - r], panel_send, cross_recv)
-
-    @pl.when(in_low)
-    def _():
-        for q in range(NQ):
-            start_to(low_at(q), scaled_v, low_v.at[tri(r) + c], panel_send, low_recv)
 
     rest = pl.ds(0, 2 * (NC - 1))
     arrived(known_v.at[rest], known_recv)
@@ -167,54 +198,42 @@
         jnp.concatenate([d_high, d_low, d_high], axis=0),
         preferred_element_type=F32,
     )
-    part_v[...] = part.astype(BF).reshape(NQ, QR, BS)
+    part = part.astype(BF)
+    high_part_v[...] = part.reshape(NQ, QR, BS)
+    low_part_v[...] = part.reshape(NL, LR, BS)
 
     @pl.when(c >= CUT)
     def _():
         for q in range(NQ):
             for i in range(SIDE):
-                start_to(high_at(q, i), part_v.at[q], pieces_v.at[c, r], part_send, part_recv)
+                start_to(high_at(q, i), high_part_v.at[q], high_pieces_v.at[c - CUT, r], part_send, part_recv)
 
     @pl.when(c < CUT)
     def _():
-        for q in range(NQ):
-            start_to(low_at(q), part_v.at[q], pieces_v.at[c, r], part_send, part_recv)
-
-    def block_copy(k, d, my_q):
-        return remote(
-            mine_v.at[k], blocks_v.at[my_q], block_send.at[k], block_recv, (r + d) % NR, k
-        )
-
-    def send_block(k, my_q, may_be_own):
+        for q in range(NL):
+            start_to(low_at(q), low_part_v.at[q], low_pieces_v.at[c, r], part_send, part_recv)
+
+    def block_copy(k, d, block, slot):
+        return remote(block, slot, block_send.at[k], block_recv, (r + d) % NR, k)
+
+    def send_block(k, block, slot, may_be_own):
         for d in range(NR):
             if d == 0 and may_be_own:
-                own = pltpu.make_async_copy(mine_v.at[k], blocks_v.at[my_q], block_recv)
+                own = pltpu.make_async_copy(block, slot, block_recv)
                 pl.when(c == k)(lambda: own.start())
-                pl.when(c != k)(lambda: block_copy(k, 0, my_q).start())
+                pl.when(c != k)(lambda: block_copy(k, 0, block, slot).start())
             else:
-                block_copy(k, d, my_q).start()
-
-    def finish_block(k, my_q, may_be_own):
+                block_copy(k, d, block, slot).start()
+
+    def finish_block(k, block, slot, may_be_own):
         for d in range(NR):
             if d == 0 and may_be_own:
-                pl.when(c != k)(lambda: block_copy(k, 0, my_q).wait_send())
+                pl.when(c != k)(lambda: block_copy(k, 0, block, slot).wait_send())
             else:
-                block_copy(k, d, my_q).wait_send()
-
-    def member(places):
-        one, which = jnp.bool_(False), jnp.int32(0)
-        for q, options in enumerate(places):
-            here = jnp.bool_(False)
-            for row, col in options:
-                here = here | ((r == row) & (c == col))
-            one, which = one | here, which + jnp.where(here, q, 0)
-        return one, which
-
-    is_high, high_q = member([[high_at(q, i) for i in range(SIDE)] for q in range(NQ)])
-    is_low, low_q = member([[low_at(q)] for q in range(NQ)])
-
-    def summed(k):
-        return jnp.sum(pieces_v[k].astype(F32), axis=0)
+                block_copy(k, d, block, slot).wait_send()
+
+    def summed(pieces):
+        return jnp.sum(pieces.astype(F32), axis=0)
 
     @pl.when(is_high)
     def _():
@@ -237,27 +256,30 @@
 
         pl.when(y < CUT - 2 * SIDE)(lambda: arrived(cross_v, cross_recv))
         pl.when(y >= CUT - 2 * SIDE)(lambda: arrived(cross_v.at[pl.ds(0, 2)], cross_recv))
-        arrived(pieces_v.at[pl.ds(CUT, TOP)], part_recv)
-        sums = [summed(k) for k in range(CUT, NB)]
+        arrived(high_pieces_v, part_recv)
+        sums = [summed(high_pieces_v[k]) for k in range(TOP)]
         done = [None] * TOP
         for j in range(TOP - 1, -1, -1):
             done[j] = sums[j].astype(BF)
-            mine_v[CUT + j] = done[j]
+            high_mine_v[j] = done[j]
             for k in range(j - 1, -1, -1):
                 sums[k] += jnp.dot(done[j], top_v[spot(CUT + j, CUT + k)], preferred_element_type=F32)
         joined = jnp.concatenate(done[::-1], axis=1)
-        low_col = (SIDE - 1 - c // SIDE) * SIDE
 
         def cross(t):
-            return remote(
-                pass_v.at[t], passed_v.at[t * SIDE + y], pass_send, pass_recv, r, low_col
-            )
+            return [
+                remote(
+                    pass_v.at[t, h], passed_v.at[t * SIDE + y], pass_send, pass_recv, r, LOW_X[h] * SIDE
+                )
+                for h in range(PER)
+            ]
 
         def send_cross(t):
             pass_v[t] = jnp.dot(
                 joined, cross_v[t].reshape(TOP * BS, BS), preferred_element_type=F32
-            )
-            cross(t).start()
+            ).reshape(PER, LR, BS)
+            for copy in cross(t):
+                copy.start()
 
         @pl.when(y < CUT - 2 * SIDE)
         def _():
@@ -265,32 +287,53 @@
 
         send_cross(1)
         send_cross(0)
+        def high_block(step, k):
+            slot = high_blocks_v.at[high_q]
+            pl.when(y == k % SIDE)(lambda: step(k, high_mine_v.at[k - CUT], slot, True))
+
         for k in range(CUT, NB):
-            pl.when(y == k % SIDE)(lambda: send_block(k, high_q, True))
-        cross(0).wait_send()
-        cross(1).wait_send()
-        pl.when(y < CUT - 2 * SIDE)(lambda: cross(2).wait_send())
+            high_block(send_block, k)
+        for t in range(2):
+            for copy in cross(t):
+                copy.wait_send()
+
+        @pl.when(y < CUT - 2 * SIDE)
+        def _():
+            for copy in cross(2):
+                copy.wait_send()
+
         for k in range(CUT, NB):
-            pl.when(y == k % SIDE)(lambda: finish_block(k, high_q, True))
+            high_block(finish_block, k)
 
     @pl.when(is_low)
     def _():
+        def low_block(step, k):
+            step(k, low_mine_v.at[k], low_blocks_v.at[low_q], k % SIDE == 0)
+
         arrived(low_v, low_recv)
-        arrived(pieces_v.at[pl.ds(0, CUT)], part_recv)
-        sums = [summed(k) for k in range(CUT)]
+        arrived(low_pieces_v, part_recv)
+        sums = [summed(low_pieces_v[k]) for k in range(CUT)]
         arrived(passed_v, pass_recv)
         sums = [sums[k] + passed_v[k] for k in range(CUT)]
         for j in range(CUT - 1, -1, -1):
             done = sums[j].astype(BF)
-            mine_v[j] = done
-            send_block(j, low_q, j in (0, SIDE))
+            low_mine_v[j] = done
             for k in range(j - 1, -1, -1):
                 sums[k] += jnp.dot(done, low_v[tri(j) + k], preferred_element_type=F32)
+        for j in range(CUT):
+            low_block(send_block, j)
         for k in range(CUT):
-            finish_block(k, low_q, k in (0, SIDE))
-
-    arrived(blocks_v, block_recv)
-    out_ref[0] = blocks_v[...].reshape(RHS, BS)
+            low_block(finish_block, k)
+
+    @pl.when(c >= CUT)
+    def _():
+        arrived(high_blocks_v, block_recv)
+        out_ref[0] = high_blocks_v[...].reshape(RHS, BS)
+
+    @pl.when(c < CUT)
+    def _():
+        arrived(low_blocks_v, block_recv)
+        out_ref[0] = low_blocks_v[...].reshape(RHS, BS)
 
     remote(known_v.at[rest], known_v.at[rest], known_send, known_recv, r, (c + 1) % NC).wait_send()
 
@@ -306,19 +349,19 @@
 
     @pl.when(in_low)
     def _():
-        for q in range(NQ):
+        for q in range(NL):
             finish_to(low_at(q), scaled_v, panel_send, low_recv)
 
     @pl.when(c >= CUT)
     def _():
         for q in range(NQ):
             for i in range(SIDE):
-                finish_to(high_at(q, i), part_v.at[q], part_send, part_recv)
+                finish_to(high_at(q, i), high_part_v.at[q], part_send, part_recv)
 
     @pl.when(c < CUT)
     def _():
-        for q in range(NQ):
-            finish_to(low_at(q), part_v.at[q], part_send, part_recv)
+        for q in range(NL):
+            finish_to(low_at(q), low_part_v.at[q], part_send, part_recv)
 
 
 def body(rhs, diag_inv, panel, offdiag, known, row_index):
@@ -338,14 +381,18 @@
             pltpu.VMEM((2 * NC, RHS, BS), BF),
             pltpu.VMEM((BS, BS), BF),
             pltpu.VMEM((NQ, QR, BS), BF),
-            pltpu.VMEM((NC, NR, QR, BS), BF),
+            pltpu.VMEM((NL, LR, BS), BF),
+            pltpu.VMEM((TOP, NR, QR, BS), BF),
+            pltpu.VMEM((CUT, NR, LR, BS), BF),
             pltpu.VMEM((tri(TOP), BS, BS), BF),
             pltpu.VMEM((3, TOP, BS, BS), BF),
             pltpu.VMEM((tri(CUT), BS, BS), BF),
-            pltpu.VMEM((NB, QR, BS), BF),
-            pltpu.VMEM((3, QR, BS), F32),
-            pltpu.VMEM((CUT, QR, BS), F32),
+            pltpu.VMEM((TOP, QR, BS), BF),
+            pltpu.VMEM((CUT, LR, BS), BF),
+            pltpu.VMEM((3, PER, LR, BS), F32),
+            pltpu.VMEM((CUT, LR, BS), F32),
             pltpu.VMEM((NQ, QR, BS), BF),
+            pltpu.VMEM((NL, LR, BS), BF),
             dma((4,)), dma, regular, regular, dma, dma,
             dma, dma, dma, dma, dma, dma,
             dma, dma, dma, dma, dma((NB,)), dma,

time: 44.7 us -> 42.3 us (0.946)
  Pallas kernels: 43.1 us -> 40.5 us
    pallas_call x1, Pallas kernels: 43.1 us -> 40.5 us  [body(): pl.pallas_call(kernel, out_shape=jax.ShapeDtypeStruct((1, RHS, BS), BF),...]
where the time goes in v3:
time: 42.3 us; the launch traced here: 41.9 us
  Pallas kernels  40.5 us (96%)
  local copies, waits for them, and re-layouts  1.32 us (3%)
    pallas_call x1, Pallas kernels, body(): pl.pallas_call(kernel, out_shape=jax.ShapeDtypeStruct((1, RHS, BS), BF),...  40.5 us
    unnamed x1, local copies, waits for them, and re-layouts  1.32 us

profile of v3, /device:TPU:1, one launch (start us, length us, event | category | flops | bytes accessed | tf_op | source)
XLA Modules:
  0.0 41.9 jit_solution(10483418613891615854)
XLA Ops:
  0.0 40.5 %shard_map.64 = bf16[1,64,128]{2,1,0:T(8,128)(2,1)} custom-call(f32[1,64,128]{2,1,0:T(8,128)} %rhs_hbm.1, f32[1,128,128]{2,1,0:T(8,128)} %dinv_hbm.1, bf16[1,1,128,128]{3,2,1,0:T(8,128)(2,1)} %panel_hbm.1, bf16[64,1,128,128]{3,2,1,0:T(8,128)(2,1)} %offdiag_hbm.1, bf16[2,64,128]{2,1,0:T(8,128)(2,1)} %known_hbm.1, s32[64]{0:T(128)} %row_index.1), custom_call_target="tpu_custom_call" | custom-call | tf_op jit(solution)/shard_map/pallas_call | solution.py:371
  40.5 1.3 %copy.8 = bf16[1,64,128]{2,1,0:T(8,128)(2,1)} copy(bf16[1,64,128]{2,1,0:T(8,128)(2,1)} %shard_map.64) | data formatting | bytes 32768

commit v4 on v3

--- a/solution.py
+++ b/solution.py
@@ -22,7 +22,7 @@
 MESH = pl.DeviceIdType.MESH
 BF = jnp.bfloat16
 F32 = jnp.float32
-SPOT_Z = (0, 1, 2, 3)
+SPOT_Z = (2, 1, 0, 7)
 HIGH_X = (3, 3, 3, 3)
 LOW_X = (0, 1)
 
@@ -42,10 +42,10 @@
 
 
 def kernel(
-    rhs_hbm, dinv_hbm, panel_hbm, offdiag_hbm, known_hbm, row_index, out_ref,
+    rhs_hbm, dinv_hbm, panel_hbm, offdiag_hbm, known_hbm, index_hbm, out_ref,
     rhs_v, dinv_v, panel_v, off_v, known_v, scaled_v,
     high_part_v, low_part_v, high_pieces_v, low_pieces_v, top_v, cross_v, low_v,
-    high_mine_v, low_mine_v, pass_v, passed_v, high_blocks_v, low_blocks_v,
+    high_mine_v, low_mine_v, pass_v, passed_v, high_blocks_v, low_blocks_v, row_index,
     load_sem, off_sem, planes_in, all_in, known_send, known_recv,
     panel_send, top_recv, cross_recv, low_recv, share_send, share_recv,
     part_send, part_recv, pass_send, pass_recv, block_send, block_recv,
@@ -106,7 +106,8 @@
     def _():
         for j in range(CUT, NB):
             for t in range(SIDE):
-                pl.when(t * SIDE + y < j)(lambda: signal(barrier, j, t * SIDE + y))
+                k = t * SIDE + y
+                pl.when((k < j) & ((r != j) | (c != k)))(lambda: signal(barrier, j, k))
 
     @pl.when(is_low)
     def _():
@@ -123,6 +124,7 @@
         pltpu.make_async_copy(dinv_hbm.at[0], dinv_v, load_sem.at[1]),
         pltpu.make_async_copy(panel_hbm.at[0, 0], panel_v, load_sem.at[2]),
         pltpu.make_async_copy(rhs_hbm.at[0], rhs_v, load_sem.at[3]),
+        pltpu.make_async_copy(index_hbm, row_index, load_sem.at[4]),
     ]
     known_load.start()
     for load in loads:
@@ -131,7 +133,8 @@
     off_load.start()
     known_load.wait()
     greeted = NC - 1 + jnp.where(c == 0, NR - 1, 0) + jnp.where(c < r, jnp.where(r < CUT, NL, NQ), 0)
-    pl.semaphore_wait(barrier, greeted - jnp.where(is_low & (c < r), 1, 0))
+    own_target = (c < r) & jnp.where(r < CUT, is_low, is_high)
+    pl.semaphore_wait(barrier, greeted - jnp.where(own_target, 1, 0))
 
     for d in (5, 15, 7, 13, 10, 9, 6, 14, 11, 2, 8, 1, 4, 3, 12):
         peer = ((c // SIDE + d // SIDE) % SIDE) * SIDE + (c + d) % SIDE
@@ -157,20 +160,25 @@
     in_cross = (r >= CUT) & (c < CUT)
     in_low = (r < CUT) & (c < r)
 
-    @pl.when(in_top)
-    def _():
-        for q in range(NQ):
-            start_to(high_at(q, y), scaled_v, top_v.at[spot(r, c)], panel_send, top_recv)
-
-    @pl.when(in_cross)
-    def _():
-        for q in range(NQ):
-            start_to(high_at(q, y), scaled_v, cross_v.at[c // SIDE, NB - 1 - r], panel_send, cross_recv)
-
-    @pl.when(in_low)
-    def _():
-        for q in range(NL):
-            start_to(low_at(q), scaled_v, low_v.at[tri(r) + c], panel_send, low_recv)
+    def send_high_panel():
+        @pl.when(in_top)
+        def _():
+            for q in range(NQ):
+                start_to(high_at(q, y), scaled_v, top_v.at[spot(r, c)], panel_send, top_recv)
+
+        @pl.when(in_cross)
+        def _():
+            for q in range(NQ):
+                start_to(high_at(q, y), scaled_v, cross_v.at[c // SIDE, NB - 1 - r], panel_send, cross_recv)
+
+    def send_low_panel():
+        @pl.when(in_low)
+        def _():
+            for q in range(NL):
+                start_to(low_at(q), scaled_v, low_v.at[tri(r) + c], panel_send, low_recv)
+
+    send_high_panel()
+    send_low_panel()
 
     @pl.when(c == 0)
     def _():
@@ -365,13 +373,17 @@
 
 
 def body(rhs, diag_inv, panel, offdiag, known, row_index):
+    operands = [
+        pltpu.with_memory_space_constraint(array, pltpu.HBM)
+        for array in (rhs, diag_inv, panel, offdiag, known, row_index)
+    ]
     anywhere = pl.BlockSpec(memory_space=pl.ANY)
     dma = pltpu.SemaphoreType.DMA
     regular = pltpu.SemaphoreType.REGULAR
     return pl.pallas_call(
         kernel,
         out_shape=jax.ShapeDtypeStruct((1, RHS, BS), BF),
-        in_specs=[anywhere] * 5 + [pl.BlockSpec(memory_space=pltpu.SMEM)],
+        in_specs=[anywhere] * 6,
         out_specs=pl.BlockSpec(memory_space=pltpu.VMEM),
         scratch_shapes=[
             pltpu.VMEM((RHS, BS), F32),
@@ -393,12 +405,13 @@
             pltpu.VMEM((CUT, LR, BS), F32),
             pltpu.VMEM((NQ, QR, BS), BF),
             pltpu.VMEM((NL, LR, BS), BF),
-            dma((4,)), dma, regular, regular, dma, dma,
+            pltpu.SMEM((TILES,), jnp.int32),
+            dma((5,)), dma, regular, regular, dma, dma,
             dma, dma, dma, dma, dma, dma,
             dma, dma, dma, dma, dma((NB,)), dma,
         ],
-        compiler_params=pltpu.CompilerParams(collective_id=0, has_side_effects=True),
-    )(rhs, diag_inv, panel, offdiag, known, row_index)
+        compiler_params=pltpu.CompilerParams(collective_id=0, has_side_effects=True, vmem_limit_bytes=24 << 20),
+    )(*operands)
 
 
 def solution(mesh):

time: 42.3 us -> 40.1 us (0.948)
  Pallas kernels: 40.5 us -> 38.8 us
  local copies, waits for them, and re-layouts: 1.32 us -> 0.61 us
    pallas_call x1, Pallas kernels: 40.5 us -> 38.8 us  [body(): pl.pallas_call(kernel, out_shape=jax.ShapeDtypeStruct((1, RHS, BS), BF),...]
    unnamed x1, local copies, waits for them, and re-layouts: 1.32 us -> 0.61 us
where the time goes in v4:
time: 40.1 us; the launch traced here: 39.4 us
  Pallas kernels  38.8 us (97%)
  local copies, waits for them, and re-layouts  0.61 us (2%)
    pallas_call x1, Pallas kernels, body(): pl.pallas_call(kernel, out_shape=jax.ShapeDtypeStruct((1, RHS, BS), BF),...  38.8 us

profile of v4, /device:TPU:1, one launch (start us, length us, event | category | flops | bytes accessed | tf_op | source)
XLA Modules:
  0.0 39.4 jit_solution(6689872500906007933)
XLA Ops:
  0.0 38.8 %shard_map.64 = bf16[1,64,128]{2,1,0:T(8,128)(2,1)S(1)} custom-call(f32[1,64,128]{2,1,0:T(8,128)} %rhs_hbm.1, f32[1,128,128]{2,1,0:T(8,128)} %dinv_hbm.1, bf16[1,1,128,128]{3,2,1,0:T(8,128)(2,1)} %panel_hbm.1, bf16[64,1,128,128]{3,2,1,0:T(8,128)(2,1)} %offdiag_hbm.1, bf16[2,64,128]{2,1,0:T(8,128)(2,1)} %known_hbm.1, s32[64]{0:T(128)} %index_hbm.1), custom_call_target="tpu_custom_call" | custom-call | tf_op jit(solution)/shard_map/pallas_call | solution.py:383
  38.8 0.6 %copy.8 = bf16[1,64,128]{2,1,0:T(8,128)(2,1)} copy(bf16[1,64,128]{2,1,0:T(8,128)(2,1)S(1)} %shard_map.64) | data formatting | bytes 32768

commit v5 on v4

--- a/solution.py
+++ b/solution.py
@@ -136,7 +136,7 @@
     own_target = (c < r) & jnp.where(r < CUT, is_low, is_high)
     pl.semaphore_wait(barrier, greeted - jnp.where(own_target, 1, 0))
 
-    for d in (5, 15, 7, 13, 10, 9, 6, 14, 11, 2, 8, 1, 4, 3, 12):
+    for d in (10, 9, 6, 14, 11, 8, 2, 5, 15, 7, 13, 1, 4, 3, 12):
         peer = ((c // SIDE + d // SIDE) % SIDE) * SIDE + (c + d) % SIDE
         remote(known_v.at[mine], known_v.at[mine], known_send, known_recv, r, peer).start()
 
@@ -262,6 +262,10 @@
                 for d in range(1, SIDE):
                     to(d).wait_send()
 
+        for i in range(SIDE):
+            if i not in {k % SIDE for k in range(CUT, NB - 1)}:
+                pl.when(y == i)(lambda: arrived(top_v, share_recv))
+
         pl.when(y < CUT - 2 * SIDE)(lambda: arrived(cross_v, cross_recv))
         pl.when(y >= CUT - 2 * SIDE)(lambda: arrived(cross_v.at[pl.ds(0, 2)], cross_recv))
         arrived(high_pieces_v, part_recv)
@@ -333,16 +337,6 @@
         for k in range(CUT):
             low_block(finish_block, k)
 
-    @pl.when(c >= CUT)
-    def _():
-        arrived(high_blocks_v, block_recv)
-        out_ref[0] = high_blocks_v[...].reshape(RHS, BS)
-
-    @pl.when(c < CUT)
-    def _():
-        arrived(low_blocks_v, block_recv)
-        out_ref[0] = low_blocks_v[...].reshape(RHS, BS)
-
     remote(known_v.at[rest], known_v.at[rest], known_send, known_recv, r, (c + 1) % NC).wait_send()
 
     @pl.when(in_top)
@@ -370,6 +364,16 @@
     def _():
         for q in range(NL):
             finish_to(low_at(q), low_part_v.at[q], part_send, part_recv)
+
+    @pl.when(c >= CUT)
+    def _():
+        arrived(high_blocks_v, block_recv)
+        out_ref[0] = high_blocks_v[...].reshape(RHS, BS)
+
+    @pl.when(c < CUT)
+    def _():
+        arrived(low_blocks_v, block_recv)
+        out_ref[0] = low_blocks_v[...].reshape(RHS, BS)
 
 
 def body(rhs, diag_inv, panel, offdiag, known, row_index):

time: 40.1 us -> 39.2 us (0.978)
  Pallas kernels: 38.8 us -> 38 us
    pallas_call x1, Pallas kernels: 38.8 us -> 38 us  [body(): pl.pallas_call(kernel, out_shape=jax.ShapeDtypeStruct((1, RHS, BS), BF),...]
where the time goes in v5:
time: 39.2 us; the launch traced here: 38.6 us
  Pallas kernels  38 us (97%)
  local copies, waits for them, and re-layouts  0.61 us (2%)
    pallas_call x1, Pallas kernels, body(): pl.pallas_call(kernel, out_shape=jax.ShapeDtypeStruct((1, RHS, BS), BF),...  38 us

profile of v5, /device:TPU:1, one launch (start us, length us, event | category | flops | bytes accessed | tf_op | source)
XLA Modules:
  0.0 38.6 jit_solution(13326511076957662360)
XLA Ops:
  0.0 38.0 %shard_map.64 = bf16[1,64,128]{2,1,0:T(8,128)(2,1)S(1)} custom-call(f32[1,64,128]{2,1,0:T(8,128)} %rhs_hbm.1, f32[1,128,128]{2,1,0:T(8,128)} %dinv_hbm.1, bf16[1,1,128,128]{3,2,1,0:T(8,128)(2,1)} %panel_hbm.1, bf16[64,1,128,128]{3,2,1,0:T(8,128)(2,1)} %offdiag_hbm.1, bf16[2,64,128]{2,1,0:T(8,128)(2,1)} %known_hbm.1, s32[64]{0:T(128)} %index_hbm.1), custom_call_target="tpu_custom_call" | custom-call | tf_op jit(solution)/shard_map/pallas_call | solution.py:387
  38.0 0.6 %copy.8 = bf16[1,64,128]{2,1,0:T(8,128)(2,1)} copy(bf16[1,64,128]{2,1,0:T(8,128)(2,1)S(1)} %shard_map.64) | data formatting | bytes 32768

commit v6 on v5

--- a/solution.py
+++ b/solution.py
@@ -212,7 +212,7 @@
 
     @pl.when(c >= CUT)
     def _():
-        for q in range(NQ):
+        for q in (3, 0, 1, 2):
             for i in range(SIDE):
                 start_to(high_at(q, i), high_part_v.at[q], high_pieces_v.at[c - CUT, r], part_send, part_recv)
 
@@ -332,8 +332,14 @@
             low_mine_v[j] = done
             for k in range(j - 1, -1, -1):
                 sums[k] += jnp.dot(done, low_v[tri(j) + k], preferred_element_type=F32)
-        for j in range(CUT):
-            low_block(send_block, j)
+        for rows in ((1, 0), (3, 2, 5, 4, 7, 6, 15, 14, 13, 12, 11, 10, 9, 8)):
+            for k in range(CUT):
+                for row in rows:
+                    copy = (low_mine_v.at[k], low_blocks_v.at[low_q], block_send.at[k], block_recv)
+                    if k % SIDE == 0 and row % 2 == 0:
+                        start_to((row, k), *copy)
+                    else:
+                        remote(*copy, row, k).start()
         for k in range(CUT):
             low_block(finish_block, k)
 

time: 39.2 us -> 38.5 us (0.982); the launches traced: 38.6 us -> 38.4 us
  no operation moved by 1% of the time
where the time goes in v6:
time: 38.5 us; the launch traced here: 38.4 us
  Pallas kernels  37.8 us (98%)
  local copies, waits for them, and re-layouts  0.61 us (2%)
    pallas_call x1, Pallas kernels, body(): pl.pallas_call(kernel, out_shape=jax.ShapeDtypeStruct((1, RHS, BS), BF),...  37.8 us

profile of v6, /device:TPU:1, one launch (start us, length us, event | category | flops | bytes accessed | tf_op | source)
XLA Modules:
  0.0 38.4 jit_solution(17462102116417336848)
XLA Ops:
  0.0 37.8 %shard_map.64 = bf16[1,64,128]{2,1,0:T(8,128)(2,1)S(1)} custom-call(f32[1,64,128]{2,1,0:T(8,128)} %rhs_hbm.1, f32[1,128,128]{2,1,0:T(8,128)} %dinv_hbm.1, bf16[1,1,128,128]{3,2,1,0:T(8,128)(2,1)} %panel_hbm.1, bf16[64,1,128,128]{3,2,1,0:T(8,128)(2,1)} %offdiag_hbm.1, bf16[2,64,128]{2,1,0:T(8,128)(2,1)} %known_hbm.1, s32[64]{0:T(128)} %index_hbm.1), custom_call_target="tpu_custom_call" | custom-call | tf_op jit(solution)/shard_map/pallas_call | solution.py:393
  37.8 0.6 %copy.8 = bf16[1,64,128]{2,1,0:T(8,128)(2,1)} copy(bf16[1,64,128]{2,1,0:T(8,128)(2,1)S(1)} %shard_map.64) | data formatting | bytes 32768

commit v7 on v6

--- a/solution.py
+++ b/solution.py
@@ -131,14 +131,13 @@
         load.start()
     off_load = pltpu.make_async_copy(offdiag_hbm.at[:, 0], off_v, off_sem)
     off_load.start()
-    known_load.wait()
     greeted = NC - 1 + jnp.where(c == 0, NR - 1, 0) + jnp.where(c < r, jnp.where(r < CUT, NL, NQ), 0)
     own_target = (c < r) & jnp.where(r < CUT, is_low, is_high)
     pl.semaphore_wait(barrier, greeted - jnp.where(own_target, 1, 0))
 
     for d in (10, 9, 6, 14, 11, 8, 2, 5, 15, 7, 13, 1, 4, 3, 12):
         peer = ((c // SIDE + d // SIDE) % SIDE) * SIDE + (c + d) % SIDE
-        remote(known_v.at[mine], known_v.at[mine], known_send, known_recv, r, peer).start()
+        remote(known_hbm, known_v.at[mine], known_send, known_recv, r, peer).start()
 
     @pl.when(c == 0)
     def _():
@@ -191,6 +190,7 @@
         pl.semaphore_wait(all_in, 1)
 
     rest = pl.ds(0, 2 * (NC - 1))
+    known_load.wait()
     arrived(known_v.at[rest], known_recv)
     off_load.wait()
     total = jnp.zeros((RHS, BS), F32)

time: 38.5 us -> 38.9 us (1.010)
  Pallas kernels: 37.8 us -> 38.2 us
where the time goes in v7:
time: 38.9 us; the launch traced here: 38.8 us
  Pallas kernels  38.2 us (98%)
  local copies, waits for them, and re-layouts  0.61 us (2%)
    pallas_call x1, Pallas kernels, body(): pl.pallas_call(kernel, out_shape=jax.ShapeDtypeStruct((1, RHS, BS), BF),...  38.2 us

profile of v7, /device:TPU:1, one launch (start us, length us, event | category | flops | bytes accessed | tf_op | source)
XLA Modules:
  0.0 38.8 jit_solution(14254298742683355365)
XLA Ops:
  0.0 38.2 %shard_map.64 = bf16[1,64,128]{2,1,0:T(8,128)(2,1)S(1)} custom-call(f32[1,64,128]{2,1,0:T(8,128)} %rhs_hbm.1, f32[1,128,128]{2,1,0:T(8,128)} %dinv_hbm.1, bf16[1,1,128,128]{3,2,1,0:T(8,128)(2,1)} %panel_hbm.1, bf16[64,1,128,128]{3,2,1,0:T(8,128)(2,1)} %offdiag_hbm.1, bf16[2,64,128]{2,1,0:T(8,128)(2,1)} %known_hbm.1, s32[64]{0:T(128)} %index_hbm.1), custom_call_target="tpu_custom_call" | custom-call | tf_op jit(solution)/shard_map/pallas_call | solution.py:393
  38.2 0.6 %copy.8 = bf16[1,64,128]{2,1,0:T(8,128)(2,1)} copy(bf16[1,64,128]{2,1,0:T(8,128)(2,1)S(1)} %shard_map.64) | data formatting | bytes 32768
